TPU v7x, 32 devices: a whole 2x2x4 slice. The times are simulated.
32 devices in a mesh: facet: 8 (over z, y), col: 4 (over x, core).
Axes of the slice: x: 2, y: 2, z: 4, core: 2. Of those that a mesh axis runs over, the one named last changes fastest.
Arguments:
- prepared: bfloat16 [8, 2, 8192, 512], P('facet', None, None, 'col'), may hold values from -6 to 6
- sub_off: int32 [8, 4], P(None, 'col'), may hold values from 0 to 8191
- fac_off: int32 [8], replicated, may hold values from 0 to 511
- win_col: int32 [4, 128], replicated, may hold values from 0 to 255
- vis_weights: bfloat16 [8, 2, 512, 512], P('facet', None, None, 'col'), may hold values from -6 to 6
Outputs:
- facet_strips: bfloat16 [8, 2, 8192, 256], P('facet', None, 'col')
All inputs are finite; a program needn't handle non-finite values.
Results may differ from a plain program's by a relative error of at most 0.0093.
Values may be sent and summed in bfloat16 or wider, within the bound.
A program may use at most 128 MiB of HBM per device.

v0:
```python
import math
import jax
import jax.numpy as jnp
from jax import lax
from jax.sharding import PartitionSpec as P

XM = 128


def taper_curve(length):
    position = (jnp.arange(length, dtype=jnp.float32) + 0.5) / length
    return 0.3 + 0.7 * jnp.sin(math.pi * position) ** 2


def phases(row_ids, col_ids, length, sign_factor, scaling):
    products = row_ids[:, None] * col_ids[None, :] % length
    angles = 2.0 * math.pi / length * products.astype(jnp.float32)
    return (jnp.cos(angles) * scaling, sign_factor * jnp.sin(angles) * scaling)


def complex_block(real_part, imag_part):
    upper_rows = jnp.concatenate([real_part, -imag_part], axis=1)
    lower_rows = jnp.concatenate([imag_part, real_part], axis=1)
    return jnp.concatenate([upper_rows, lower_rows], axis=0).astype(jnp.bfloat16)


def small_tables(length):
    positions = jnp.arange(length, dtype=jnp.int32)
    taper_vals = taper_curve(length)
    fwd_re, fwd_im = phases(positions, positions, length, -1.0, 1.0 / math.sqrt(length))
    back_re, back_im = phases(positions, positions, length, 1.0, 1.0 / math.sqrt(length))
    forward = complex_block(fwd_re * taper_vals[None, :], fwd_im * taper_vals[None, :])
    backward = complex_block(back_re * taper_vals[:, None], back_im * taper_vals[:, None])
    return (forward, backward)


def grid_tables(length, facet_count, contrib_len):
    positions = jnp.arange(length, dtype=jnp.int32)
    fwd_re, fwd_im = phases(
        positions, positions, length, -1.0, 1.0 / math.sqrt(facet_count * contrib_len)
    )
    back_re, back_im = phases(positions, positions, length, 1.0, 1.0 / math.sqrt(length))
    return (complex_block(fwd_re, fwd_im), complex_block(back_re, back_im))


def finish_map(columns, out_cols):
    frequency = jnp.arange(out_cols, dtype=jnp.int32)
    products = columns[:, None] * frequency[None, :] % out_cols
    angles = 2.0 * math.pi / out_cols * products.astype(jnp.float32)
    scaling = 1.0 / math.sqrt(2 * out_cols)
    real_part = jnp.cos(angles) * scaling
    imag_part = jnp.sin(angles) * scaling
    from_real = jnp.concatenate([real_part, imag_part], axis=1)
    from_imag = jnp.concatenate([-imag_part, real_part], axis=1)
    return jnp.stack([from_real, from_imag], axis=0).astype(jnp.bfloat16)


def apply_weights(spectrum, weights):
    spec_re = spectrum[..., 0, :, :]
    spec_im = spectrum[..., 1, :, :]
    weight_re = weights[..., 0, :, :].astype(jnp.float32)
    weight_im = weights[..., 1, :, :].astype(jnp.float32)
    joined = jnp.stack(
        [weight_re * spec_re - weight_im * spec_im, weight_re * spec_im + weight_im * spec_re],
        axis=-3,
    )
    return joined.astype(jnp.bfloat16)


def body(prepared, sub_off, fac_off, win_col, vis_weights):
    facet_count = fac_off.shape[0]
    group_count = lax.axis_size("facet")
    per_device = vis_weights.shape[0]
    grid_len = vis_weights.shape[2]
    facet_strip = prepared[0]
    facet_len = facet_strip.shape[1]
    strip_width = facet_strip.shape[2]
    window_pos = jnp.arange(XM, dtype=jnp.int32)
    forward_small, backward_small = small_tables(XM)
    forward_grid, backward_grid = grid_tables(grid_len, facet_count, XM)
    starts = sub_off[:, 0].reshape(group_count, per_device).T
    src_rows = (starts[:, :, None] + window_pos[None, None, :]) % facet_len
    picked = (
        facet_strip[:, src_rows]
        .transpose(1, 2, 0, 3, 4)
        .reshape(per_device, group_count, 2 * XM, strip_width)
    )
    payload = jnp.einsum(
        "ab,sfbc->sfac", forward_small, picked, preferred_element_type=jnp.float32
    ).astype(jnp.bfloat16)
    arrived = lax.all_to_all(payload, "facet", split_axis=1, concat_axis=1, tiled=True)
    dest_rows = ((fac_off[:, None] + window_pos[None, :]) % grid_len).reshape(-1)
    placement = (dest_rows[None, :] == jnp.arange(grid_len, dtype=jnp.int32)[:, None]).astype(
        jnp.bfloat16
    )
    flat_rows = arrived.reshape(per_device, facet_count, 2, XM, strip_width).transpose(
        0, 2, 1, 3, 4
    )
    flat_rows = flat_rows.reshape(per_device, 2, facet_count * XM, strip_width)
    assembled = jnp.einsum(
        "rq,spqc->sprc", placement, flat_rows, preferred_element_type=jnp.float32
    ).astype(jnp.bfloat16)
    spectrum = jnp.einsum(
        "ab,sbc->sac",
        forward_grid,
        assembled.reshape(per_device, 2 * grid_len, strip_width),
        preferred_element_type=jnp.float32,
    )
    weighted = apply_weights(spectrum.reshape(per_device, 2, grid_len, strip_width), vis_weights)
    grid_image = jnp.einsum(
        "ab,sbc->sac",
        backward_grid,
        weighted.reshape(per_device, 2 * grid_len, strip_width),
        preferred_element_type=jnp.float32,
    )
    grid_image = grid_image.astype(jnp.bfloat16).reshape(per_device, 2, grid_len, strip_width)
    back_rows = (
        grid_image[:, :, dest_rows]
        .reshape(per_device, 2, facet_count, XM, strip_width)
        .transpose(0, 2, 1, 3, 4)
    )
    back_rows = back_rows.reshape(per_device, facet_count, 2 * XM, strip_width)
    returned = lax.all_to_all(back_rows, "facet", split_axis=1, concat_axis=1, tiled=True)
    item_count = per_device * group_count
    returned_terms = jnp.einsum(
        "ab,sfbc->sfac", backward_small, returned, preferred_element_type=jnp.float32
    )
    returned_terms = returned_terms.reshape(item_count, 2, XM, strip_width)
    item_starts = starts.reshape(-1)
    row_shift = item_starts % XM
    block_ids = item_starts // XM
    block_count = facet_len // XM
    padded_terms = jnp.concatenate([returned_terms, jnp.zeros_like(returned_terms)], axis=2)
    frames = jax.vmap(lambda term, amount: jnp.roll(term, amount, axis=1))(padded_terms, row_shift)
    frames = frames.reshape(item_count, 2, 2, XM, strip_width)
    block_range = jnp.arange(block_count, dtype=jnp.int32)[:, None]
    lower_hits = (block_ids[None, :] == block_range).astype(jnp.float32)
    upper_hits = (((block_ids + 1) % block_count)[None, :] == block_range).astype(jnp.float32)
    accum = jnp.einsum(
        "bs,spyc->pbyc", lower_hits, frames[:, :, 0], precision=lax.Precision.HIGHEST
    )
    accum = accum + jnp.einsum(
        "bs,spyc->pbyc", upper_hits, frames[:, :, 1], precision=lax.Precision.HIGHEST
    )
    strip_sum = accum.reshape(2, facet_len, strip_width).astype(jnp.bfloat16)
    col_count = lax.axis_size("col")
    out_cols = strip_width * col_count // 2
    own_rows = facet_len // col_count
    all_maps = jax.vmap(lambda columns: finish_map(columns, out_cols))(win_col)
    moved_rows = lax.all_to_all(strip_sum, "col", split_axis=1, concat_axis=0, tiled=True)
    moved_rows = moved_rows.reshape(col_count, 2, own_rows, strip_width)
    summed = jnp.einsum("cpyk,cpkm->ym", moved_rows, all_maps, preferred_element_type=jnp.float32)
    result = summed.astype(jnp.bfloat16).reshape(own_rows, 2, out_cols).transpose(1, 0, 2)
    return result.reshape(1, 2, own_rows, out_cols)


def solution(mesh):
    in_specs = (
        P("facet", None, None, "col"),
        P(None, "col"),
        P(),
        P(),
        P("facet", None, None, "col"),
    )
    out_specs = P("facet", None, "col", None)
    return jax.shard_map(body, mesh=mesh, in_specs=in_specs, out_specs=out_specs, check_vma=False)
```

profile of v0, /device:TPU:0, one launch (start us, length us, event | category | flops | bytes accessed | tf_op | source)
XLA Modules:
  0.0 197.0 jit_solution(260517381722625866)
XLA Ops:
  0.0 0.1 broadcast_multiply_fusion
  0.1 0.1 broadcast_multiply_fusion.1
  0.1 0.0 copy-start.3
  0.1 10.1 %copy.72 = bf16[1,2,8192,128]{3,1,2,0:T(2,128)(2,1)} copy(bf16[1,2,8192,128]{3,2,1,0:T(8,128)(2,1)} %param.5) | data formatting | bytes 8388608 | tf_op args[0]
  10.2 0.0 copy-done.3
  10.2 0.1 fusion.88
  10.3 0.0 copy-start.2
  10.3 5.9 %gather_fusion = bf16[1024,2,128]{2,1,0:T(2,128)(2,1)S(1)} fusion(bf16[2,8192,128]{2,0,1:T(2,128)(2,1)} %bitcast.141, s32[1024]{0:T(1024)S(1)} %fusion.88), kind=kCustom, calls=%fused_computation | custom fusion | bytes 1052672 | tf_op jit(solution)/shard_map/gather | solution.py:84
  16.2 2.1 %copy.33 = bf16[1,8,2,128,128]{3,2,4,1,0:T(2,128)(2,1)S(1)} copy(bf16[1,8,2,128,128]{4,2,3,1,0:T(2,128)(2,1)S(1)} %bitcast.144) | data formatting | bytes 1048576 | tf_op jit(solution)/shard_map/transpose | solution.py:85
  18.3 0.3 reshape.349
  18.6 0.3 negate_convert_fusion.3
  18.9 1.1 fusion.25
  20.1 7.3 %all-to-all-start = ((bf16[1,8,256,128]{2,3,0,1:T(8,128)(2,1)}), bf16[1,8,256,128]{2,3,0,1:T(8,128)(2,1)S(1)}, u32[]{:S(2)}, u32[]{:S(2)}) async-start(bf16[1,8,256,128]{2,3,0,1:T(8,128)(2,1)} %fusion.25), calls=%async_computation | async-start | bytes 1048576 | tf_op jit(solution)/shard_map/all_to_all | solution.py:91
  27.4 5.2 %negate_convert_fusion.1 = (bf16[512,512]{1,0:T(8,128)(2,1)S(1)}, bf16[512,512]{1,0:T(8,128)(2,1)}) fusion(), kind=kLoop, calls=%fused_computation.52 | loop fusion | flops 4980736 | bytes 1048576 | tf_op jit(solution)/shard_map/convert.27
  32.6 4.6 %multiply_convert_fusion.3 = bf16[512,512]{1,0:T(8,128)(2,1)} fusion(), kind=kLoop, calls=%fused_computation.59 | loop fusion | flops 4194304 | bytes 524288 | tf_op jit(solution)/shard_map/convert.24
  37.2 4.4 %negate_convert_fusion = (bf16[512,512]{1,0:T(8,128)(2,1)S(1)}, bf16[512,512]{1,0:T(8,128)(2,1)S(1)}) fusion(), kind=kLoop, calls=%fused_computation.50 | loop fusion | flops 4980736 | bytes 1048576 | tf_op jit(solution)/shard_map/convert.19
  41.6 4.0 %multiply_convert_fusion.2 = bf16[512,512]{1,0:T(8,128)(2,1)S(1)} fusion(), kind=kLoop, calls=%fused_computation.58 | loop fusion | flops 4194304 | bytes 524288 | tf_op jit(solution)/shard_map/convert.16
  45.6 0.0 copy-done.2
  45.6 0.1 add_select_fusion.3
  45.7 0.1 iota_add_fusion
  45.8 0.0 all-to-all-done
  45.8 0.1 reshape.350
  46.0 0.3 copy.73
  46.3 0.2 reshape.351
  46.5 0.6 fusion.35
  47.1 0.2 copy.36
  47.3 0.0 copy-start
  47.3 2.2 %fusion.26 = f32[1,1024,128]{1,2,0:T(8,128)S(1)} fusion(bf16[1024,128]{1,0:T(8,128)(2,1)S(1)} %bitcast.148, bf16[512,512]{1,0:T(8,128)(2,1)} %get-tuple-element.25, bf16[512,512]{1,0:T(8,128)(2,1)} %multiply_convert_fusion.3, bf16[512,512]{1,0:T(8,128)(2,1)S(1)} %get-tuple-element.24), kind=kOutput, calls=%fused_computation.36 | convolution fusion | flops 276824064 | bytes 2359296 | tf_op jit(solution)/shard_map/ab,sbc->sac/dot_general | solution.py:103
  49.5 0.2 copy.57
  49.7 0.0 copy-done
  49.7 0.1 fusion.62
  49.9 0.8 fusion.38
  50.7 0.2 reshape.370
  50.9 0.4 copy.39
  51.3 3.7 %gather_fusion.1 = bf16[1024,2,128]{2,1,0:T(2,128)(2,1)S(1)} fusion(bf16[2,512,128]{2,0,1:T(2,128)(2,1)S(1)} %copy.39, s32[1024]{0:T(1024)S(1)} %broadcast_clamp_fusion), kind=kCustom, calls=%fused_computation.1 | custom fusion | bytes 1052672 | tf_op jit(solution)/shard_map/gather | solution.py:118
  55.0 2.1 %copy.40 = bf16[1,8,2,128,128]{3,2,4,1,0:T(2,128)(2,1)S(1)} copy(bf16[1,8,2,128,128]{4,2,3,1,0:T(2,128)(2,1)S(1)} %bitcast.145) | data formatting | bytes 1048576 | tf_op jit(solution)/shard_map/transpose | solution.py:120
  57.1 1.1 reshape.356
  58.2 6.0 %all-to-all-start.1 = ((bf16[1,8,256,128]{2,3,0,1:T(8,128)(2,1)}), bf16[1,8,256,128]{2,3,0,1:T(8,128)(2,1)S(1)}, u32[]{:S(2)}, u32[]{:S(2)}) async-start(bf16[1,8,256,128]{2,3,0,1:T(8,128)(2,1)} %reshape.356), calls=%async_computation.1 | async-start | bytes 1048576 | tf_op jit(solution)/shard_map/all_to_all | solution.py:123
  64.2 13.9 %all-to-all-done.1 = bf16[1,8,256,128]{2,3,0,1:T(8,128)(2,1)S(1)} async-done(((bf16[1,8,256,128]{2,3,0,1:T(8,128)(2,1)}), bf16[1,8,256,128]{2,3,0,1:T(8,128)(2,1)S(1)}, u32[]{:S(2)}, u32[]{:S(2)}) %all-to-all-start.1) | async-done | bytes 524320 | tf_op jit(solution)/shard_map/all_to_all | solution.py:123
  78.2 0.3 convolution_bitcast_fusion
  78.5 0.5 reshape.358
  79.0 1.4 copy.41
  80.5 0.3 broadcast_in_dim.3
  80.8 3.5 %pad_maximum_fusion = f32[8,2,512,128]{3,1,0,2:T(2,128)} fusion(f32[8,2,128,128]{3,1,0,2:T(2,128)S(1)} %broadcast_in_dim.3, f32[8,2,128,128]{3,1,0,2:T(2,128)S(1)} %copy.41), kind=kLoop, calls=%fused_computation.5 | loop fusion | flops 3145728 | bytes 6291456 | tf_op jit(solution)/shard_map/vmap(jit(_roll_dynamic))/concatenate | solution.py:134
  84.3 5.6 %gather_fusion.2 = f32[8,2,256,128]{3,1,2,0:T(2,128)S(1)} fusion(f32[8,2,512,128]{3,1,0,2:T(2,128)} %pad_maximum_fusion, s32[8]{0:T(128)S(1)} %or_bitcast_fusion), kind=kCustom, calls=%fused_computation.2 | custom fusion | bytes 4194432 | tf_op jit(solution)/shard_map/vmap(jit(_roll_dynamic))/gather | solution.py:134
  89.9 0.2 copy.43
  90.1 0.2 fusion.108
  90.3 3.6 %fusion.46 = f32[2,128,128,64]{2,3,1,0:T(8,128)S(1)} fusion(f32[8,2,1,128,128]{4,3,2,1,0:T(8,128)S(1)} %get-tuple-element.8, s32[8]{0:T(128)S(1)} %get-tuple-element.6), kind=kOutput, calls=%fused_computation.49 | convolution fusion | flops 201327104 | bytes 9437216 | tf_op jit(solution)/shard_map/bs,spyc->pbyc/dot_general | solution.py:139
  93.9 4.7 %fusion = bf16[2,64,128,128]{3,1,2,0:T(8,128)(2,1)S(1)} fusion(f32[2,128,128,64]{2,3,1,0:T(8,128)S(1)} %fusion.46, f32[8,2,1,128,128]{4,3,2,1,0:T(8,128)S(1)} %get-tuple-element.7, s32[8]{0:T(128)S(1)} %get-tuple-element.5), kind=kOutput, calls=%fused_computation.4 | convolution fusion | flops 205521408 | bytes 13631520 | tf_op jit(solution)/shard_map/bs,spyc->pbyc/dot_general | solution.py:142
  98.6 2.7 %copy.46 = bf16[2,64,128,128]{3,2,1,0:T(8,128)(2,1)S(1)} copy(bf16[2,64,128,128]{3,1,2,0:T(8,128)(2,1)S(1)} %fusion) | data formatting | bytes 8388608 | tf_op jit(solution)/shard_map/convert_element_type | solution.py:145
  101.3 35.5 %copy.47 = bf16[2,8192,128]{2,0,1:T(2,128)(2,1)} copy(bf16[2,8192,128]{2,1,0:T(8,128)(2,1)S(1)} %bitcast.139) | data formatting | bytes 8388608 | tf_op jit(solution)/shard_map/convert_element_type | solution.py:145
  136.8 0.0 copy-start.1
  136.8 5.0 %all-to-all-start.2 = ((bf16[2,8192,128]{2,0,1:T(2,128)(2,1)}), bf16[2,8192,128]{2,0,1:T(2,128)(2,1)}, u32[]{:S(2)}, u32[]{:S(2)}) async-start(bf16[2,8192,128]{2,0,1:T(2,128)(2,1)} %copy.47), calls=%async_computation.2 | async-start | bytes 8388608 | tf_op jit(solution)/shard_map/all_to_all | solution.py:150
  141.8 0.0 copy-done.1
  141.8 2.3 %fusion.60 = (bf16[4,128,256]{1,2,0:T(8,128)(2,1)S(1)}, bf16[4,128,256]{1,2,0:T(8,128)(2,1)S(1)}, bf16[4,128,256]{1,2,0:T(8,128)(2,1)S(1)}) fusion(s32[4,128]{1,0:T(4,128)S(1)} %copy-done.1), kind=kLoop, calls=%fused_computation.78 | loop fusion | flops 2621440 | bytes 788480 | tf_op jit(solution)/shard_map/convert.7
  144.1 0.1 maximum_bitcast_fusion.2
  144.1 45.8 %all-to-all-done.2 = bf16[2,8192,128]{2,0,1:T(2,128)(2,1)} async-done(((bf16[2,8192,128]{2,0,1:T(2,128)(2,1)}), bf16[2,8192,128]{2,0,1:T(2,128)(2,1)}, u32[]{:S(2)}, u32[]{:S(2)}) %all-to-all-start.2) | async-done | bytes 4194336 | tf_op jit(solution)/shard_map/all_to_all | solution.py:150
  190.0 4.6 %bitcast_convert_fusion = bf16[2048,512]{0,1:T(8,128)(2,1)S(1)} fusion(bf16[2,4,2048,128]{3,0,2,1:T(2,128)(2,1)} %bitcast.41, bf16[1,4,128,512]{2,3,0,1:T(8,128)(2,1)S(1)} %get-tuple-element.12, bf16[1,4,128,512]{2,3,0,1:T(8,128)(2,1)S(1)} %get-tuple-element.11), kind=kOutput, calls=%fused_computation.6 | convolution fusion | flops 2149056512 | bytes 7340032 | tf_op jit(solution)/shard_map/cpyk,cpkm->ym/dot_general | solution.py:152
  194.5 2.5 %copy.51 = bf16[2048,2,256]{2,0,1:T(8,128)(2,1)} copy(bf16[2048,2,256]{0,2,1:T(8,128)(2,1)S(1)} %bitcast.142) | data formatting | bytes 4194304 | tf_op jit(solution)/shard_map/reshape | solution.py:153
  (5 shorter events, 0.1 us)
Async XLA Ops:
  0.1 10.1 %copy-start.3 = (s32[8,1]{0,1:T(1,128)S(1)}, s32[8,1]{0,1:T(1,128)}, u32[]{:S(2)}) copy-start(s32[8,1]{0,1:T(1,128)} %param.6) | copy-start | bytes 100
  10.3 35.3 %copy-start.2 = (s32[8]{0:T(128)S(1)}, s32[8]{0:T(128)}, u32[]{:S(2)}) copy-start(s32[8]{0:T(128)} %param.7) | copy-start | bytes 100
  20.1 25.8 %all-to-all-start = ((bf16[1,8,256,128]{2,3,0,1:T(8,128)(2,1)}), bf16[1,8,256,128]{2,3,0,1:T(8,128)(2,1)S(1)}, u32[]{:S(2)}, u32[]{:S(2)}) async-start(bf16[1,8,256,128]{2,3,0,1:T(8,128)(2,1)} %fusion.25), calls=%async_computation | async-start | bytes 1048576 | tf_op jit(solution)/shard_map/all_to_all | solution.py:91
  47.3 2.4 %copy-start = (bf16[1,2,512,128]{3,2,1,0:T(8,128)(2,1)S(1)}, bf16[1,2,512,128]{3,2,1,0:T(8,128)(2,1)}, u32[]{:S(2)}) copy-start(bf16[1,2,512,128]{3,2,1,0:T(8,128)(2,1)} %param.9) | copy-start | bytes 786436
  58.2 20.0 %all-to-all-start.1 = ((bf16[1,8,256,128]{2,3,0,1:T(8,128)(2,1)}), bf16[1,8,256,128]{2,3,0,1:T(8,128)(2,1)S(1)}, u32[]{:S(2)}, u32[]{:S(2)}) async-start(bf16[1,8,256,128]{2,3,0,1:T(8,128)(2,1)} %reshape.356), calls=%async_computation.1 | async-start | bytes 1048576 | tf_op jit(solution)/shard_map/all_to_all | solution.py:123
  136.8 5.0 %copy-start.1 = (s32[4,128]{1,0:T(4,128)S(1)}, s32[4,128]{1,0:T(4,128)}, u32[]{:S(2)}) copy-start(s32[4,128]{1,0:T(4,128)} %param.8) | copy-start | bytes 6148
  136.8 53.2 %all-to-all-start.2 = ((bf16[2,8192,128]{2,0,1:T(2,128)(2,1)}), bf16[2,8192,128]{2,0,1:T(2,128)(2,1)}, u32[]{:S(2)}, u32[]{:S(2)}) async-start(bf16[2,8192,128]{2,0,1:T(2,128)(2,1)} %copy.47), calls=%async_computation.2 | async-start | bytes 8388608 | tf_op jit(solution)/shard_map/all_to_all | solution.py:150
where the time goes:
time: 198 us; the launch traced here: 197 us
  local copies, waits for them, and re-layouts  75.8 us (38%)
  waiting for transfers between devices  59.8 us (30%)
  other arithmetic  24.9 us (13%)
  starting transfers between devices  18.3 us (9%)
  matrix products  17.9 us (9%)
    all_to_all x1, waiting for transfers between devices, body(): lax.all_to_all(strip_sum, 'col', split_axis=1, concat_axis=0, tiled=True)  45.8 us
    convert_element_type x2, local copies, waits for them, and re-layouts, body(): strip_sum = accum.reshape(2, facet_len, strip_width).astype(jnp.bfloat16)  38.2 us
    another operation x7, other arithmetic  20.9 us
    all_to_all x1, waiting for transfers between devices, body(): lax.all_to_all(back_rows, 'facet', split_axis=1, concat_axis=1, tiled=True)  13.9 us
    unnamed x9, local copies, waits for them, and re-layouts  10.1 us
    all_to_all x1, starting transfers between devices, body(): lax.all_to_all(payload, 'facet', split_axis=1, concat_axis=1, tiled=True)  7.31 us
    all_to_all x1, starting transfers between devices, body(): lax.all_to_all(back_rows, 'facet', split_axis=1, concat_axis=1, tiled=True)  6 us
    gather x1, local copies, waits for them, and re-layouts, body(): facet_strip[:, src_rows].transpose(1, 2, 0, 3, 4)  5.88 us
  transfers between devices with their start and end apart: 3, of which 2 were waited for; matrix products, arithmetic and copies ran while one was open for 11% of the time, Pallas kernels for 0%

commit v1 on v0

--- a/solution.py
+++ b/solution.py
@@ -120,7 +120,12 @@
         .transpose(0, 2, 1, 3, 4)
     )
     back_rows = back_rows.reshape(per_device, facet_count, 2 * XM, strip_width)
-    returned = lax.all_to_all(back_rows, "facet", split_axis=1, concat_axis=1, tiled=True)
+    returned = jnp.concatenate(
+        lax.all_to_all(
+            jnp.stack(jnp.split(back_rows, lax.axis_size("facet"), axis=1)), "facet", 0, 0
+        ),
+        axis=1,
+    )
     item_count = per_device * group_count
     returned_terms = jnp.einsum(
         "ab,sfbc->sfac", backward_small, returned, preferred_element_type=jnp.float32

time: 198 us -> 202 us (1.020)
  local copies, waits for them, and re-layouts: 75.8 us -> 80.1 us
    unnamed x9 -> x16, local copies, waits for them, and re-layouts: 10.1 us -> 14.6 us
  transfers between devices with their start and end apart: 3 -> 3, of which waited for: 2 -> 2; matrix products, arithmetic and copies ran while one was open for 11% -> 10% of each run, Pallas kernels for 0% -> 0%
where the time goes in v1:
time: 202 us; the launch traced here: 201 us
  local copies, waits for them, and re-layouts  80.1 us (40%)
  waiting for transfers between devices  59.7 us (30%)
  other arithmetic  25.1 us (12%)
  starting transfers between devices  18.3 us (9%)
  matrix products  17.9 us (9%)
    all_to_all x1, waiting for transfers between devices, body(): lax.all_to_all(strip_sum, 'col', split_axis=1, concat_axis=0, tiled=True)  45.8 us
    convert_element_type x2, local copies, waits for them, and re-layouts, body(): strip_sum = accum.reshape(2, facet_len, strip_width).astype(jnp.bfloat16)  38.2 us
    another operation x7, other arithmetic  20.4 us
    unnamed x16, local copies, waits for them, and re-layouts  14.6 us
    all_to_all x1, waiting for transfers between devices, body(): lax.all_to_all(jnp.stack(jnp.split(back_rows, lax.axis_size('facet'), axi...  13.9 us
    all_to_all x1, starting transfers between devices, body(): lax.all_to_all(payload, 'facet', split_axis=1, concat_axis=1, tiled=True)  7.31 us
    all_to_all x1, starting transfers between devices, body(): lax.all_to_all(jnp.stack(jnp.split(back_rows, lax.axis_size('facet'), axi...  6 us
    gather x1, local copies, waits for them, and re-layouts, body(): facet_strip[:, src_rows].transpose(1, 2, 0, 3, 4)  5.88 us
  transfers between devices with their start and end apart: 3, of which 2 were waited for; matrix products, arithmetic and copies ran while one was open for 10% of the time, Pallas kernels for 0%

profile of v1, /device:TPU:0, one launch (start us, length us, event | category | flops | bytes accessed | tf_op | source)
XLA Modules:
  0.0 201.4 jit_solution(16626790836156814063)
XLA Ops:
  0.0 0.1 broadcast_multiply_fusion
  0.1 0.1 broadcast_multiply_fusion.1
  0.1 0.7 iota_add_fusion
  0.9 0.0 copy-start.3
  0.9 10.1 %copy.86 = bf16[1,2,8192,128]{3,1,2,0:T(2,128)(2,1)} copy(bf16[1,2,8192,128]{3,2,1,0:T(8,128)(2,1)} %param.5) | data formatting | bytes 8388608 | tf_op args[0]
  11.0 0.0 copy-done.3
  11.0 0.1 fusion.96
  11.1 5.9 %gather_fusion = bf16[1024,2,128]{2,1,0:T(2,128)(2,1)S(1)} fusion(bf16[2,8192,128]{2,0,1:T(2,128)(2,1)} %bitcast.173, s32[1024]{0:T(1024)S(1)} %get-tuple-element.22), kind=kCustom, calls=%fused_computation | custom fusion | bytes 1052672 | tf_op jit(solution)/shard_map/gather | solution.py:84
  17.0 2.1 %copy.47 = bf16[1,8,2,128,128]{3,2,4,1,0:T(2,128)(2,1)S(1)} copy(bf16[1,8,2,128,128]{4,2,3,1,0:T(2,128)(2,1)S(1)} %bitcast.176) | data formatting | bytes 1048576 | tf_op jit(solution)/shard_map/transpose | solution.py:85
  19.0 0.3 reshape.351
  19.4 0.3 negate_convert_fusion.3
  19.7 1.1 fusion.25
  20.8 7.3 %all-to-all-start = ((bf16[1,8,256,128]{2,3,0,1:T(8,128)(2,1)}), bf16[1,8,256,128]{2,3,0,1:T(8,128)(2,1)S(1)}, u32[]{:S(2)}, u32[]{:S(2)}) async-start(bf16[1,8,256,128]{2,3,0,1:T(8,128)(2,1)} %fusion.25), calls=%async_computation | async-start | bytes 1048576 | tf_op jit(solution)/shard_map/all_to_all | solution.py:91
  28.1 4.0 %multiply_convert_fusion.3 = bf16[512,512]{1,0:T(8,128)(2,1)S(1)} fusion(), kind=kLoop, calls=%fused_computation.59 | loop fusion | flops 4194304 | bytes 524288 | tf_op jit(solution)/shard_map/convert.24
  32.1 4.0 %multiply_convert_fusion.2 = bf16[512,512]{1,0:T(8,128)(2,1)S(1)} fusion(), kind=kLoop, calls=%fused_computation.58 | loop fusion | flops 4194304 | bytes 524288 | tf_op jit(solution)/shard_map/convert.16
  36.1 5.4 %negate_convert_fusion.1 = (bf16[512,512]{1,0:T(8,128)(2,1)}, bf16[512,512]{1,0:T(8,128)(2,1)}) fusion(), kind=kLoop, calls=%fused_computation.52 | loop fusion | flops 4980736 | bytes 1048576 | tf_op jit(solution)/shard_map/convert.27
  41.5 4.4 %negate_convert_fusion = (bf16[512,512]{1,0:T(8,128)(2,1)S(1)}, bf16[512,512]{1,0:T(8,128)(2,1)S(1)}) fusion(), kind=kLoop, calls=%fused_computation.50 | loop fusion | flops 4980736 | bytes 1048576 | tf_op jit(solution)/shard_map/convert.19
  45.9 0.0 copy-done.2
  45.9 0.1 add_select_fusion.3
  46.0 0.0 all-to-all-done
  46.0 0.1 reshape.352
  46.1 0.3 copy.87
  46.5 0.2 reshape.353
  46.7 0.6 fusion.35
  47.3 0.2 copy.50
  47.4 0.0 copy-start
  47.4 2.2 %fusion.26 = f32[1,1024,128]{1,2,0:T(8,128)S(1)} fusion(bf16[1024,128]{1,0:T(8,128)(2,1)S(1)} %bitcast.180, bf16[512,512]{1,0:T(8,128)(2,1)} %get-tuple-element.27, bf16[512,512]{1,0:T(8,128)(2,1)S(1)} %multiply_convert_fusion.3, bf16[512,512]{1,0:T(8,128)(2,1)} %get-tuple-element.26), kind=kOutput, calls=%fused_computation.36 | convolution fusion | flops 276824064 | bytes 2359296 | tf_op jit(solution)/shard_map/ab,sbc->sac/dot_general | solution.py:103
  49.7 0.2 copy.71
  49.9 0.0 copy-done
  49.9 0.1 fusion.62
  50.0 0.8 fusion.38
  50.8 0.2 reshape.372
  51.0 0.4 copy.53
  51.4 3.7 %gather_fusion.1 = bf16[1024,2,128]{2,1,0:T(2,128)(2,1)S(1)} fusion(bf16[2,512,128]{2,0,1:T(2,128)(2,1)S(1)} %copy.53, s32[1024]{0:T(1024)S(1)} %get-tuple-element.23), kind=kCustom, calls=%fused_computation.1 | custom fusion | bytes 1052672 | tf_op jit(solution)/shard_map/gather | solution.py:118
  55.1 2.1 %copy.54 = bf16[1,8,2,128,128]{3,2,4,1,0:T(2,128)(2,1)S(1)} copy(bf16[1,8,2,128,128]{4,2,3,1,0:T(2,128)(2,1)S(1)} %bitcast.177) | data formatting | bytes 1048576 | tf_op jit(solution)/shard_map/transpose | solution.py:120
  57.2 0.3 reshape.358
  57.5 0.6 fusion.87
  58.2 0.6 fusion.86
  58.8 0.6 fusion.85
  59.4 0.6 fusion.84
  60.1 0.6 fusion.83
  60.7 0.6 fusion.82
  61.3 0.6 fusion.81
  62.0 0.6 fusion.80
  62.6 6.0 %all-to-all-start.1 = ((bf16[8,1,1,256,128]{3,4,2,1,0:T(8,128)(2,1)}), bf16[8,1,1,256,128]{3,4,2,1,0:T(8,128)(2,1)S(1)}, u32[]{:S(2)}, u32[]{:S(2)}) async-start(bf16[8,1,1,256,128]{3,4,2,1,0:T(8,128)(2,1)} %fusion.80), calls=%async_computation.1 | async-start | bytes 1048576 | tf_op jit(solution)/shard_map/all_to_all | solution.py:124
  68.7 13.9 %all-to-all-done.1 = bf16[8,1,1,256,128]{3,4,2,1,0:T(8,128)(2,1)S(1)} async-done(((bf16[8,1,1,256,128]{3,4,2,1,0:T(8,128)(2,1)}), bf16[8,1,1,256,128]{3,4,2,1,0:T(8,128)(2,1)S(1)}, u32[]{:S(2)}, u32[]{:S(2)}) %all-to-all-start.1) | async-done | bytes 524320 | tf_op jit(solution)/shard_map/all_to_all | solution.py:124
  82.6 0.3 convolution_bitcast_fusion
  82.9 0.5 reshape.360
  83.5 1.4 copy.55
  84.9 0.3 broadcast_in_dim.3
  85.2 3.5 %pad_maximum_fusion = f32[8,2,512,128]{3,1,0,2:T(2,128)} fusion(f32[8,2,128,128]{3,1,0,2:T(2,128)S(1)} %broadcast_in_dim.3, f32[8,2,128,128]{3,1,0,2:T(2,128)S(1)} %copy.55), kind=kLoop, calls=%fused_computation.5 | loop fusion | flops 3145728 | bytes 6291456 | tf_op jit(solution)/shard_map/vmap(jit(_roll_dynamic))/concatenate | solution.py:139
  88.7 5.6 %gather_fusion.2 = f32[8,2,256,128]{3,1,2,0:T(2,128)S(1)} fusion(f32[8,2,512,128]{3,1,0,2:T(2,128)} %pad_maximum_fusion, s32[8]{0:T(128)S(1)} %or_bitcast_fusion), kind=kCustom, calls=%fused_computation.2 | custom fusion | bytes 4194432 | tf_op jit(solution)/shard_map/vmap(jit(_roll_dynamic))/gather | solution.py:139
  94.3 0.2 copy.57
  94.5 0.2 fusion.116
  94.7 3.6 %fusion.46 = f32[2,128,128,64]{2,3,1,0:T(8,128)S(1)} fusion(f32[8,2,1,128,128]{4,3,2,1,0:T(8,128)S(1)} %get-tuple-element.8, s32[8]{0:T(128)S(1)} %get-tuple-element.6), kind=kOutput, calls=%fused_computation.49 | convolution fusion | flops 201327104 | bytes 9437216 | tf_op jit(solution)/shard_map/bs,spyc->pbyc/dot_general | solution.py:144
  98.3 4.7 %fusion = bf16[2,64,128,128]{3,1,2,0:T(8,128)(2,1)S(1)} fusion(f32[2,128,128,64]{2,3,1,0:T(8,128)S(1)} %fusion.46, f32[8,2,1,128,128]{4,3,2,1,0:T(8,128)S(1)} %get-tuple-element.7, s32[8]{0:T(128)S(1)} %get-tuple-element.5), kind=kOutput, calls=%fused_computation.4 | convolution fusion | flops 205521408 | bytes 13631520 | tf_op jit(solution)/shard_map/bs,spyc->pbyc/dot_general | solution.py:147
  103.0 2.7 %copy.60 = bf16[2,64,128,128]{3,2,1,0:T(8,128)(2,1)S(1)} copy(bf16[2,64,128,128]{3,1,2,0:T(8,128)(2,1)S(1)} %fusion) | data formatting | bytes 8388608 | tf_op jit(solution)/shard_map/convert_element_type | solution.py:150
  105.7 35.5 %copy.61 = bf16[2,8192,128]{2,0,1:T(2,128)(2,1)} copy(bf16[2,8192,128]{2,1,0:T(8,128)(2,1)S(1)} %bitcast.171) | data formatting | bytes 8388608 | tf_op jit(solution)/shard_map/convert_element_type | solution.py:150
  141.2 5.0 %all-to-all-start.2 = ((bf16[2,8192,128]{2,0,1:T(2,128)(2,1)}), bf16[2,8192,128]{2,0,1:T(2,128)(2,1)}, u32[]{:S(2)}, u32[]{:S(2)}) async-start(bf16[2,8192,128]{2,0,1:T(2,128)(2,1)} %copy.61), calls=%async_computation.2 | async-start | bytes 8388608 | tf_op jit(solution)/shard_map/all_to_all | solution.py:155
  146.2 2.3 %fusion.60 = (bf16[4,128,256]{1,2,0:T(8,128)(2,1)S(1)}, bf16[4,128,256]{1,2,0:T(8,128)(2,1)S(1)}, bf16[4,128,256]{1,2,0:T(8,128)(2,1)S(1)}) fusion(s32[4,128]{1,0:T(4,128)S(1)} %copy-done.1), kind=kLoop, calls=%fused_computation.78 | loop fusion | flops 2621440 | bytes 788480 | tf_op jit(solution)/shard_map/convert.7
  148.5 0.1 maximum_bitcast_fusion.2
  148.5 45.8 %all-to-all-done.2 = bf16[2,8192,128]{2,0,1:T(2,128)(2,1)} async-done(((bf16[2,8192,128]{2,0,1:T(2,128)(2,1)}), bf16[2,8192,128]{2,0,1:T(2,128)(2,1)}, u32[]{:S(2)}, u32[]{:S(2)}) %all-to-all-start.2) | async-done | bytes 4194336 | tf_op jit(solution)/shard_map/all_to_all | solution.py:155
  194.4 4.6 %bitcast_convert_fusion = bf16[2048,512]{0,1:T(8,128)(2,1)S(1)} fusion(bf16[2,4,2048,128]{3,0,2,1:T(2,128)(2,1)} %bitcast.49, bf16[1,4,128,512]{2,3,0,1:T(8,128)(2,1)S(1)} %get-tuple-element.12, bf16[1,4,128,512]{2,3,0,1:T(8,128)(2,1)S(1)} %get-tuple-element.11), kind=kOutput, calls=%fused_computation.6 | convolution fusion | flops 2149056512 | bytes 7340032 | tf_op jit(solution)/shard_map/cpyk,cpkm->ym/dot_general | solution.py:157
  198.9 2.5 %copy.65 = bf16[2048,2,256]{2,0,1:T(8,128)(2,1)} copy(bf16[2048,2,256]{0,2,1:T(8,128)(2,1)S(1)} %bitcast.174) | data formatting | bytes 4194304 | tf_op jit(solution)/shard_map/reshape | solution.py:158
  (7 shorter events, 0.1 us)
Async XLA Ops:
  0.9 10.1 %copy-start.3 = (s32[8,1]{0,1:T(1,128)S(1)}, s32[8,1]{0,1:T(1,128)}, u32[]{:S(2)}) copy-start(s32[8,1]{0,1:T(1,128)} %param.6) | copy-start | bytes 100
  11.1 34.8 %copy-start.2 = (s32[8]{0:T(128)S(1)}, s32[8]{0:T(128)}, u32[]{:S(2)}) copy-start(s32[8]{0:T(128)} %param.7) | copy-start | bytes 100
  20.8 25.2 %all-to-all-start = ((bf16[1,8,256,128]{2,3,0,1:T(8,128)(2,1)}), bf16[1,8,256,128]{2,3,0,1:T(8,128)(2,1)S(1)}, u32[]{:S(2)}, u32[]{:S(2)}) async-start(bf16[1,8,256,128]{2,3,0,1:T(8,128)(2,1)} %fusion.25), calls=%async_computation | async-start | bytes 1048576 | tf_op jit(solution)/shard_map/all_to_all | solution.py:91
  47.4 2.4 %copy-start = (bf16[1,2,512,128]{3,2,1,0:T(8,128)(2,1)S(1)}, bf16[1,2,512,128]{3,2,1,0:T(8,128)(2,1)}, u32[]{:S(2)}) copy-start(bf16[1,2,512,128]{3,2,1,0:T(8,128)(2,1)} %param.9) | copy-start | bytes 786436
  62.6 20.0 %all-to-all-start.1 = ((bf16[8,1,1,256,128]{3,4,2,1,0:T(8,128)(2,1)}), bf16[8,1,1,256,128]{3,4,2,1,0:T(8,128)(2,1)S(1)}, u32[]{:S(2)}, u32[]{:S(2)}) async-start(bf16[8,1,1,256,128]{3,4,2,1,0:T(8,128)(2,1)} %fusion.80), calls=%async_computation.1 | async-start | bytes 1048576 | tf_op jit(solution)/shard_map/all_to_all | solution.py:124
  141.2 5.0 %copy-start.1 = (s32[4,128]{1,0:T(4,128)S(1)}, s32[4,128]{1,0:T(4,128)}, u32[]{:S(2)}) copy-start(s32[4,128]{1,0:T(4,128)} %param.8) | copy-start | bytes 6148
  141.2 53.2 %all-to-all-start.2 = ((bf16[2,8192,128]{2,0,1:T(2,128)(2,1)}), bf16[2,8192,128]{2,0,1:T(2,128)(2,1)}, u32[]{:S(2)}, u32[]{:S(2)}) async-start(bf16[2,8192,128]{2,0,1:T(2,128)(2,1)} %copy.61), calls=%async_computation.2 | async-start | bytes 8388608 | tf_op jit(solution)/shard_map/all_to_all | solution.py:155
